TPU v7x, 32 devices: a whole 2x2x4 slice. The times are simulated.
32 devices in a mesh: segment: 4 (over y, x), bins: 8 (over z, core).
Axes of the slice: x: 2, y: 2, z: 4, core: 2. Of those that a mesh axis runs over, the one named last changes fastest.
Arguments:
- cube_train: bfloat16 [2, 512, 256, 256], P(None, None, ('segment', 'bins')), may hold values from -6 to 6
- cube_apply: bfloat16 [2, 512, 256, 256], P(None, None, ('segment', 'bins')), may hold values from -6 to 6
- hard_bins: int32 [8], replicated, may hold values from 1 to 511, as said below
- easy_bins: int32 [16], replicated, may hold values from 0 to 510, as said below
- stagger: int32 [8, 2], replicated, may hold values from 0 to 127, as said below
- hard_gates: int32 [8, 64], P('bins'), may hold values from 0 to 255, as said below
- easy_gates: int32 [16, 64], P('bins'), may hold values from 0 to 255, as said below
Outputs:
- hard_beams: float32 [8, 2, 256, 128], P('bins', None, 'segment')
- easy_beams: float32 [16, 2, 256, 128], P('bins', None, 'segment')
Inputs may be any that keep to these rules, and one draw needn't show every extreme that they name: `hard_bins`: 8 distinct bins, none of them among easy_bins. `easy_bins`: 16 distinct bins, none of them among hard_bins. `stagger`: in each row the second offset is larger than the first. `hard_gates`: each row holds 64 distinct range gates. `easy_gates`: each row holds 64 distinct range gates.
All inputs are finite; a program needn't handle non-finite values.
Results may differ from a plain program's by a relative error of at most 0.005.
Values may be sent and summed in bfloat16 or wider, within the bound.
A program may use at most 64 MiB of HBM per device.

v0:
```python
import jax
import jax.numpy as jnp
from jax import lax
from jax.experimental import pallas as pl
from jax.experimental.pallas import tpu as pltpu
from jax.sharding import PartitionSpec as P

BEAMS = 128
STEPS = 6


LOADING = 0.5
TWO_PI = 6.283185307179586
MESH = pl.DeviceIdType.MESH


def doppler_table(hard_bins, easy_bins, stagger, pulses, groups):
    zeros = jnp.zeros((groups,), jnp.int32)
    bin_row = jnp.stack([hard_bins, hard_bins, easy_bins[0::2], easy_bins[1::2]], axis=1).reshape(
        -1
    )
    offset_row = jnp.stack([stagger[:, 0], stagger[:, 1], zeros, zeros], axis=1).reshape(-1)
    pulse = jnp.arange(pulses, dtype=jnp.int32)
    lagged = pulse[None, :] - offset_row[:, None]
    valid = lagged >= 0
    lagged = jnp.where(valid, lagged, 0)
    phase = (bin_row[:, None] * lagged % pulses).astype(jnp.float32) * (TWO_PI / pulses)
    taper = 0.54 - 0.46 * jnp.cos(lagged.astype(jnp.float32) * (TWO_PI / pulses))
    amplitude = jnp.where(valid, taper, jnp.zeros_like(taper)) * 0.0625
    real_part = amplitude * jnp.cos(phase)
    imag_part = -amplitude * jnp.sin(phase)
    upper = jnp.concatenate([real_part, -imag_part], axis=1)
    lower = jnp.concatenate([imag_part, real_part], axis=1)
    return jnp.concatenate([upper, lower], axis=0).astype(jnp.bfloat16)


def steering(beam_index, bin_value, offsets, channels, beams, pulses):
    channel = jnp.arange(channels, dtype=jnp.int32)
    spatial = (channel[:, None] * (beam_index[None, :] + beams // 2) % beams).astype(
        jnp.float32
    ) * (TWO_PI / beams)
    angles = []
    for offset in offsets:
        temporal = (bin_value * offset % pulses).astype(jnp.float32) * (TWO_PI / pulses)
        angles.append(spatial + temporal)
    angle = jnp.concatenate(angles, axis=0)
    scale = 1.0 / jnp.sqrt(jnp.float32(len(offsets) * channels))
    return jnp.concatenate([jnp.cos(angle), jnp.sin(angle)], axis=0) * scale


def chebyshev_solve(snapshot, steer, steps):
    train = snapshot.shape[0]
    order = snapshot.shape[1] // 2
    gram = jnp.dot(snapshot.T, snapshot, preferred_element_type=jnp.float32)
    real_cov = (gram[:order, :order] + gram[order:, order:]) / train
    imag_cov = (gram[:order, order:] - gram[order:, :order]) / train
    trace = jnp.trace(real_cov)
    loading = LOADING * trace / order
    upper = jnp.concatenate([real_cov, -imag_cov], axis=1)
    lower = jnp.concatenate([imag_cov, real_cov], axis=1)
    operator = jnp.concatenate([upper, lower], axis=0) + loading * jnp.eye(
        2 * order, dtype=gram.dtype
    )
    highest = loading + trace
    theta = (highest + loading) / 2.0
    delta = (highest - loading) / 2.0
    sigma = theta / delta
    rho = 1.0 / sigma
    weights = jnp.zeros_like(steer)
    resid = steer
    direction = steer / theta
    for step in range(steps):
        weights = weights + direction
        resid = resid - jnp.dot(operator, direction, precision=lax.Precision.HIGHEST)
        if step + 1 < steps:
            rho_next = 1.0 / (2.0 * sigma - rho)
            direction = rho_next * rho * direction + 2.0 * rho_next / delta * resid
            rho = rho_next
    return weights


def group_weights(snap, hard_bin, offsets, beam_index, channels, beams, pulses, steps):
    train = snap.shape[2]
    hard_snap = jnp.transpose(snap[:, 0:2], (2, 0, 1, 3)).reshape(train, 4 * channels)
    hard_steer = steering(beam_index, hard_bin, offsets, channels, beams, pulses)
    hard_w = chebyshev_solve(hard_snap, hard_steer, steps).astype(jnp.bfloat16)
    parts = [hard_w.reshape(2, 2, channels, -1)]
    zero_offset = jnp.zeros((), jnp.int32)
    easy_steer = steering(beam_index, hard_bin, [zero_offset], channels, beams, pulses)
    for kind in (2, 3):
        easy_snap = jnp.transpose(snap[:, kind], (1, 0, 2)).reshape(train, 2 * channels)
        easy_w = chebyshev_solve(easy_snap, easy_steer, steps).astype(jnp.bfloat16)
        parts.append(easy_w.reshape(2, 1, channels, -1))
    return jnp.concatenate(parts, axis=1)


def beamform(spectra, weights):
    swapped = jnp.stack([spectra[1], -spectra[0]])
    stacked = jnp.stack([spectra, swapped])
    hard_part = jnp.einsum(
        "ozkrc,zkcb->orb", stacked[:, :, 0:2], weights[:, 0:2], preferred_element_type=jnp.float32
    )
    easy_first = jnp.einsum(
        "ozrc,zcb->orb", stacked[:, :, 2], weights[:, 2], preferred_element_type=jnp.float32
    )
    easy_second = jnp.einsum(
        "ozrc,zcb->orb", stacked[:, :, 3], weights[:, 3], preferred_element_type=jnp.float32
    )
    return jnp.stack([hard_part, easy_first, easy_second])


def select_gates(gate_rows, block):
    count = block.shape[2]
    positions = jnp.arange(count, dtype=jnp.int32)
    onehot = (gate_rows[:, :, None] == positions[None, None, :]).astype(jnp.bfloat16)
    return jnp.einsum("ktr,zkrc->zktc", onehot, block, preferred_element_type=jnp.float32)


def route_spectra(table, cube, groups):
    pulses = cube.shape[1]
    flat = cube.reshape(2 * pulses, -1)
    spectra = jnp.dot(table, flat, preferred_element_type=jnp.float32).astype(jnp.bfloat16)
    spectra = spectra.reshape(2, groups, 4, cube.shape[2], cube.shape[3])
    routed = lax.all_to_all(spectra, "bins", split_axis=1, concat_axis=3, tiled=True)
    return routed[:, 0]


def per_device(cube_train, cube_apply, hard_bins, easy_bins, stagger, hard_gates, easy_gates):
    groups = lax.axis_size("bins")
    sections = lax.axis_size("segment")
    section = lax.axis_index("segment")
    group = lax.axis_index("bins")
    pulses = cube_train.shape[1]
    channels = cube_train.shape[3]
    beams_local = BEAMS // sections
    table = doppler_table(hard_bins, easy_bins, stagger, pulses, groups)
    block_train = route_spectra(table, cube_train, groups)
    gate_rows = jnp.concatenate([hard_gates, hard_gates, easy_gates], axis=0)
    snap = select_gates(gate_rows, lax.all_gather(block_train, "segment", axis=2, tiled=True))
    snap = snap.astype(jnp.bfloat16)
    beam_index = section * beams_local + jnp.arange(beams_local, dtype=jnp.int32)
    offsets = [stagger[group, 0], stagger[group, 1]]
    weights = group_weights(
        snap, hard_bins[group], offsets, beam_index, channels, BEAMS, pulses, STEPS
    )
    block_apply = route_spectra(table, cube_apply, groups)
    partial_out = beamform(lax.all_gather(block_apply, "segment", axis=2, tiled=True), weights)
    outputs = lax.all_to_all(
        partial_out.astype(jnp.bfloat16), "segment", split_axis=2, concat_axis=3, tiled=True
    ).astype(partial_out.dtype)
    return (outputs[0:1], outputs[1:3])


def cos512(turn):
    folded = 128 - jnp.abs(turn - 256)
    x = folded.astype(jnp.float32) * (TWO_PI / 512)
    y = x * x
    p = -2.5052108e-8 * y + 2.7557319e-6
    p = p * y - 1.9841270e-4
    p = p * y + 8.3333333e-3
    p = p * y - 1.6666667e-1
    return -(x + x * y * p)


def split(value):
    high = value.astype(jnp.bfloat16)
    return high, (value - high.astype(jnp.float32)).astype(jnp.bfloat16)


def dual_coefficients(order):
    loading = LOADING / order
    theta = 0.5 + loading
    sigma = 2.0 * theta
    rho = 1.0 / sigma
    a, c, alpha = 1.0 / theta, 1.0, 0.0
    steps = []
    for step in range(STEPS):
        alpha += a
        c -= loading * a
        if step + 1 < STEPS:
            rho_next = 1.0 / (2.0 * sigma - rho)
            steps.append((a, rho_next * rho, 4.0 * rho_next))
            a = rho_next * rho * a + 4.0 * rho_next * c
            rho = rho_next
    return loading, alpha, steps


def dot32(left, right, dims):
    return lax.dot_general(left, right, (dims, ((), ())), preferred_element_type=jnp.float32)


PIECES = ((0, 1), (2,), (3,))


def multiply(left, right):
    return (
        jnp.dot(left[0], right[0], preferred_element_type=jnp.float32)
        + jnp.dot(left[0], right[1], preferred_element_type=jnp.float32)
        + jnp.dot(left[1], right[0], preferred_element_type=jnp.float32)
    )


def rotated(real, imag, turn):
    return real * turn[0] - imag * turn[1], real * turn[1] + imag * turn[0]


def solve(kinds, order, gram, look):
    identity = lax.broadcasted_iota(jnp.int32, (128, 128), 0) == lax.broadcasted_iota(
        jnp.int32, (128, 128), 1
    )
    diagonal_sum = jnp.sum(jnp.where(identity, gram, 0.0), axis=1, keepdims=True)
    inverse = 1.0 / (jnp.sum(diagonal_sum, axis=0, keepdims=True) * (0.5 / 64))
    loading, alpha, steps = dual_coefficients(order)
    look = look * (inverse * (1.0 / (64 * order**0.5)))
    resid = -steps[0][0] * look
    move = steps[0][2] * resid
    return dict(
        kinds=kinds, order=order, gram=split(gram * (inverse * (1.0 / 64))), look=look,
        inverse=inverse, loading=loading, alpha=alpha, steps=steps,
        resid=resid, move=move, total=move,
    )


def advance(state, step):
    a, keep, gain = state["steps"][step]
    change = (
        a * state["look"]
        + state["loading"] * state["move"]
        + multiply(state["gram"], split(state["move"]))
    )
    state["resid"] = state["resid"] - change
    state["move"] = keep * state["move"] + gain * state["resid"]
    state["total"] = state["total"] + state["move"]


def fused_kernel(
    train_hbm, apply_hbm, settings, hard_out, easy_out,
    cubes, expanded, upper0, upper1, upper2, upper3, lower0, lower1, lower2, lower3,
    spectra, arrived_a, arrived_b, arrived_c, received_a, received_b,
    part_a, part_b, part_c, inbox_a, inbox_b, inbox_c,
    merged_a, merged_b, merged_c, final_a, final_b, final_c,
    load_sem, send_sem, recv_sem, swap_send, swap_recv,
):
    section = lax.axis_index("segment")
    group = lax.axis_index("bins")
    groups = 8
    across = section + 1 - 2 * (section % 2)
    along = (section + 2) % 4
    lhs = ((upper0, upper1, upper2, upper3), (lower0, lower1, lower2, lower3))
    loads = []
    for which, source in enumerate((train_hbm, apply_hbm)):
        for k in range(4):
            rows = pl.ds(2048 * k, 2048)
            copy = pltpu.make_async_copy(
                source.at[rows], cubes.at[which, rows], load_sem.at[which, k]
            )
            copy.start()
            loads.append(copy)
    barrier = pltpu.get_barrier_semaphore()
    for offset in range(1, groups):
        pl.semaphore_signal(
            barrier, inc=1, device_id=(section, (group + offset) % groups), device_id_type=MESH
        )
    for other in (across, along):
        pl.semaphore_signal(barrier, inc=1, device_id=(other, group), device_id_type=MESH)

    block = (
        lax.broadcasted_iota(jnp.int32, (16, 128), 1) // 8
        == lax.broadcasted_iota(jnp.int32, (16, 128), 0)
    ).astype(jnp.float32).astype(jnp.bfloat16)
    nothing = jnp.zeros((16, 128), jnp.bfloat16)
    spread = jnp.concatenate(
        [
            jnp.concatenate([nothing] * j + [block] + [nothing] * (15 - j), axis=1)
            for j in range(16)
        ],
        axis=0,
    )
    pair = lax.broadcasted_iota(jnp.int32, (64, 128), 0) // 2
    bin_col = jnp.zeros((64, 128), jnp.int32)
    lag_col = jnp.zeros((64, 128), jnp.int32)
    for j in range(groups):
        for t in range(4):
            here = pair == 16 * (t // 2) + 2 * j + t % 2
            bin_col = jnp.where(here, settings[0, j] if t < 2 else settings[1, 2 * j + t - 2], bin_col)
            if t < 2:
                lag_col = jnp.where(here, settings[2 + t, j], lag_col)
    bin_col = jnp.concatenate([bin_col] * 4, axis=1)
    lag_col = jnp.concatenate([lag_col] * 4, axis=1)
    lagged = lax.broadcasted_iota(jnp.int32, (64, 512), 1) - lag_col
    valid = lagged >= 0
    lagged = jnp.where(valid, lagged, 0)
    turn = (bin_col * lagged) & 511
    quarter = (lax.broadcasted_iota(jnp.int32, (64, 512), 0) % 2) * 128
    amplitude = jnp.where(valid, 0.54 - 0.46 * cos512(lagged), 0.0) * 0.0625
    first = (amplitude * cos512((turn + quarter) & 511)).astype(jnp.bfloat16)
    second = (amplitude * cos512((turn + quarter + 384) & 511)).astype(jnp.bfloat16)
    stacked = jnp.concatenate(
        [first[:, :256], first[:, 256:], second[:, :256], second[:, 256:]], axis=0
    )
    expanded[...] = jnp.dot(stacked, spread, preferred_element_type=jnp.float32)
    diagonal = (lax.broadcasted_iota(jnp.int32, (16, 2048), 0) % 8) == (
        lax.broadcasted_iota(jnp.int32, (16, 2048), 1) % 8
    )

    def fill(part, k):
        for i in range(16):
            row = 64 * k + 32 * part + 2 * i
            upper = jnp.broadcast_to(expanded[row : row + 1, :], (8, 2048))
            lower = jnp.broadcast_to(expanded[row + 1 : row + 2, :], (8, 2048))
            both = jnp.where(diagonal, jnp.concatenate([upper, lower], axis=0), 0.0)
            lhs[part][k][16 * i : 16 * i + 16, :] = both.astype(jnp.bfloat16)

    arrived = (arrived_a, arrived_b, arrived_c)
    sends = [[], [], [], [], []]

    def scatter(which, index, start, rows, landing):
        here = pl.ds(pl.multiple_of(rows * group, rows), rows)
        for offset in range(1, groups):
            target = (group + offset) % groups
            copy = pltpu.make_async_remote_copy(
                src_ref=spectra.at[which, pl.ds(pl.multiple_of(32 * target + start, 16), rows)],
                dst_ref=landing.at[here],
                send_sem=send_sem.at[index, offset],
                recv_sem=recv_sem.at[index, offset],
                device_id=(section, target),
                device_id_type=MESH,
            )
            copy.start()
            sends[index].append(copy)
        landing[here, :] = spectra[which, pl.ds(pl.multiple_of(32 * group + start, 16), rows), :]

    def transform(which, part):
        total = None
        for k in range(4):
            if part == 0:
                loads[4 * which + k].wait()
            product = jnp.dot(
                lhs[part][k][...], cubes[which, 2048 * k : 2048 * k + 2048, :],
                preferred_element_type=jnp.float32,
            )
            total = product if total is None else total + product
        spectra[which, 256 * part : 256 * part + 256, :] = total.astype(jnp.bfloat16)

    for k in range(4):
        fill(0, k)
    transform(0, 0)
    pl.semaphore_wait(barrier, groups + 1)
    scatter(0, 0, 0, 32, arrived_a)
    for k in range(4):
        fill(1, k)
    transform(0, 1)
    scatter(0, 1, 256, 16, arrived_b)
    scatter(0, 2, 272, 16, arrived_c)
    transform(1, 0)
    scatter(1, 3, 0, 32, received_a)
    transform(1, 1)
    scatter(1, 4, 256, 32, received_b)

    lane = lax.broadcasted_iota(jnp.int32, (1, 128), 1) % 64
    lists = [jnp.zeros((1, 128), jnp.int32)] * 3
    for i in range(64):
        here = lane == i
        lists = [
            jnp.where(here, value, row)
            for value, row in zip((settings[4, i], settings[5, i], settings[6, i]), lists)
        ]
    gates = (lists[0], lists[0], lists[1], lists[2])
    selects = []
    for kinds in PIECES:
        count = len(kinds)
        side = 128 * count
        gate_row = jnp.concatenate([gates[t] for t in kinds], axis=1) - 64 * section
        column = lax.broadcasted_iota(jnp.int32, (1, side), 1)
        wanted = (
            (gate_row // 8) * (16 * count) + (column // 64 % count) * 16
            + (column // (64 * count)) * 8 + gate_row % 8
        )
        wanted = jnp.where((gate_row >= 0) & (gate_row < 64), wanted, -1)
        onehot = lax.broadcasted_iota(jnp.int32, (side, side), 0) == wanted
        selects.append(jnp.transpose(onehot.astype(jnp.float32)).astype(jnp.bfloat16))

    parts, inboxes = (part_a, part_b, part_c), (inbox_a, inbox_b, inbox_c)
    merges, finals = (merged_a, merged_b, merged_c), (final_a, final_b, final_c)
    swaps = {}

    def swap(stage, index, origin, target):
        half_rows = 64 * len(PIECES[index])
        swaps[stage, index] = []
        for half in range(2):
            rows = pl.ds(half_rows * half, half_rows)
            copy = pltpu.make_async_remote_copy(
                src_ref=origin.at[rows],
                dst_ref=target.at[rows],
                send_sem=swap_send.at[index, 2 * stage + half],
                recv_sem=swap_recv.at[index, 2 * stage + half],
                device_id=((across, along)[(half + stage) % 2], group),
                device_id_type=MESH,
            )
            copy.start()
            swaps[stage, index].append(copy)

    channel = lax.broadcasted_iota(jnp.int32, (256, 128), 0)
    beam = lax.broadcasted_iota(jnp.int32, (256, 128), 1)
    place = ((channel * (beam + 64)) & 127) * 4
    steer_real = cos512(place)
    steer_imag = cos512((place + 384) & 511)
    steer_high, steer_low = split(jnp.concatenate([steer_real, steer_imag], axis=1))
    rotations = []
    for half in range(2):
        angle = jnp.full((8, 128), (settings[0, group] * settings[2 + half, group]) & 511, jnp.int32)
        rotations.append((cos512(angle)[0:1], cos512((angle + 384) & 511)[0:1]))

    for index in range(3):
        for copy in sends[index]:
            copy.wait_recv()
        parts[index][...] = jnp.dot(
            selects[index], arrived[index][...], preferred_element_type=jnp.float32
        ).astype(jnp.bfloat16)
        swap(0, index, parts[index], inboxes[index])
    for index in range(3):
        for copy in swaps[0, index]:
            copy.wait_recv()
        merges[index][...] = parts[index][...] + inboxes[index][...]
        swap(1, index, merges[index], finals[index])

    weights = [None] * 4
    for indices in ((0,), (1, 2)):
        states, mixers = [], {}
        for index in indices:
            for copy in swaps[1, index]:
                copy.wait_recv()
        for index in indices:
            kinds = PIECES[index]
            snapshot = merges[index][...] + finals[index][...]
            seen = jnp.dot(snapshot, steer_high, preferred_element_type=jnp.float32) + jnp.dot(
                snapshot, steer_low, preferred_element_type=jnp.float32
            )
            half = 64 * len(kinds)
            gram, look = None, None
            for i, t in enumerate(kinds):
                real_rows, imag_rows = slice(64 * i, 64 * i + 64), slice(half + 64 * i, half + 64 * i + 64)
                real, imag = snapshot[real_rows], snapshot[imag_rows]
                upper = jnp.concatenate([real, -imag], axis=1)
                lower = jnp.concatenate([imag, real], axis=1)
                mixers[t] = jnp.concatenate([upper, lower], axis=0)
                from_real, from_imag = seen[real_rows], seen[imag_rows]
                look_real = from_real[:, :128] - from_imag[:, 128:]
                look_imag = from_real[:, 128:] + from_imag[:, :128]
                if t < 2:
                    look_real, look_imag = rotated(look_real, look_imag, rotations[t])
                one_look = jnp.concatenate([look_real, look_imag], axis=0)
                one_gram = dot32(mixers[t], mixers[t], ((1,), (1,)))
                look = one_look if look is None else look + one_look
                gram = one_gram if gram is None else gram + one_gram
            states.append(solve(kinds, 256 * len(kinds), gram, look))
        for step in range(1, STEPS - 1):
            for state in states:
                advance(state, step)
        for state in states:
            high, low = split(state["total"])
            for t in state["kinds"]:
                lift = dot32(mixers[t], high, ((0,), (0,))) + dot32(mixers[t], low, ((0,), (0,)))
                base = steer_real, steer_imag
                if t < 2:
                    base = rotated(*base, rotations[t])
                scale = state["alpha"] / state["order"] ** 0.5
                weights[t] = jnp.concatenate(
                    [
                        (lift[:256] + scale * base[0]) * state["inverse"],
                        (lift[256:] + scale * base[1]) * state["inverse"],
                    ],
                    axis=1,
                ).astype(jnp.bfloat16)

    for copy in sends[3] + sends[4]:
        copy.wait_recv()
    products = []
    for t in range(4):
        rows = jnp.concatenate(
            [
                (received_a, received_b)[t // 2][32 * b + 16 * (t % 2) : 32 * b + 16 * (t % 2) + 16, :]
                for b in range(groups)
            ],
            axis=0,
        )
        products.append(jnp.dot(rows, weights[t], preferred_element_type=jnp.float32))
    for out, at, product in (
        (hard_out, 0, products[0] + products[1]),
        (easy_out, 0, products[2]),
        (easy_out, 1, products[3]),
    ):
        for b in range(groups):
            from_real = product[16 * b : 16 * b + 8]
            from_imag = product[16 * b + 8 : 16 * b + 16]
            out[at, 0, 8 * b : 8 * b + 8, :] = from_real[:, :128] + from_imag[:, 128:]
            out[at, 1, 8 * b : 8 * b + 8, :] = from_imag[:, :128] - from_real[:, 128:]
    for copies in (*sends, *swaps.values()):
        for copy in copies:
            copy.wait_send()


def fused_device(cube_train, cube_apply, hard_bins, easy_bins, stagger, hard_gates, easy_gates):
    bf16, f32 = jnp.bfloat16, jnp.float32
    smem = pl.BlockSpec(memory_space=pltpu.SMEM)
    vmem = pl.BlockSpec(memory_space=pltpu.VMEM)
    settings = sum(
        jnp.pad(rows, ((above, 7 - above - rows.shape[0]), (0, 128 - rows.shape[1])))
        for above, rows in (
            (0, hard_bins[None]), (1, easy_bins[None]), (2, stagger.T), (4, hard_gates),
            (5, easy_gates),
        )
    )
    held = [pltpu.VMEM((rows, 256), bf16) for rows in (256, 128, 128)]
    return pl.pallas_call(
        fused_kernel,
        out_shape=(
            jax.ShapeDtypeStruct((1, 2, 64, 128), f32),
            jax.ShapeDtypeStruct((2, 2, 64, 128), f32),
        ),
        in_specs=[pl.BlockSpec(memory_space=pltpu.HBM)] * 2 + [smem],
        out_specs=(vmem, vmem),
        scratch_shapes=[
            pltpu.VMEM((2, 8192, 256), bf16),
            pltpu.VMEM((256, 2048), f32),
            *[pltpu.VMEM((256, 2048), bf16)] * 8,
            pltpu.VMEM((2, 512, 256), bf16),
            *held,
            pltpu.VMEM((256, 256), bf16),
            pltpu.VMEM((256, 256), bf16),
            *held, *held, *held, *held,
            pltpu.SemaphoreType.DMA((2, 4)),
            pltpu.SemaphoreType.DMA((5, 8)),
            pltpu.SemaphoreType.DMA((5, 8)),
            pltpu.SemaphoreType.DMA((3, 4)),
            pltpu.SemaphoreType.DMA((3, 4)),
        ],
        compiler_params=pltpu.CompilerParams(
            collective_id=0, has_side_effects=True, vmem_limit_bytes=52 * 1024 * 1024
        ),
    )(
        cube_train.reshape(8192, 256), cube_apply.reshape(8192, 256),
        settings,
    )


def dispatch(cube_train, cube_apply, hard_bins, easy_bins, stagger, hard_gates, easy_gates):
    small = (
        lax.axis_size("bins") == 8
        and lax.axis_size("segment") == 4
        and cube_train.shape == (2, 512, 8, 256)
        and hard_gates.shape == (1, 64)
    )
    run = fused_device if small else per_device
    return run(cube_train, cube_apply, hard_bins, easy_bins, stagger, hard_gates, easy_gates)


def solution(mesh):
    in_specs = (
        P(None, None, ("segment", "bins"), None),
        P(None, None, ("segment", "bins"), None),
        P(),
        P(),
        P(),
        P("bins", None),
        P("bins", None),
    )
    out_specs = (P("bins", None, "segment", None), P("bins", None, "segment", None))
    return jax.shard_map(
        dispatch, mesh=mesh, in_specs=in_specs, out_specs=out_specs, check_vma=False
    )
```

profile of v0, /device:TPU:0, one launch (start us, length us, event | category | flops | bytes accessed | tf_op | source)
XLA Modules:
  0.0 28.7 jit_solution(11721012160514930645)
XLA Ops:
  0.6 0.7 %pad_add_fusion.settings = s32[7,128]{1,0:T(8,128)S(1)} fusion(s32[2,64]{1,0:T(2,128)} %param.13, s32[1,64]{1,0:T(1,128)} %param.12, s32[2,8]{1,0:T(2,128)} %bitcast.7, s32[1,16]{1,0:T(1,128)} %bitcast.8, s32[1,8]{1,0:T(1,128)} %bitcast.9), kind=kLoop, calls=%fused_computation | loop fusion | flops 3584 | bytes 4512 | tf_op jit(solution)/shard_map/add | solution.py:507
  1.4 26.0 %shard_map.86 = (f32[1,2,64,128]{3,2,1,0:T(8,128)S(1)}, f32[2,2,64,128]{3,2,1,0:T(8,128)S(1)}) custom-call(bf16[8192,256]{1,0:T(8,128)(2,1)} %bitcast.5, bf16[8192,256]{1,0:T(8,128)(2,1)} %bitcast.6, s32[7,128]{1,0:T(8,128)S(1)} %pad_add_fusion.settings), custom_call_target="tpu_custom_call" | custom-call | tf_op jit(solution)/shard_map/pallas_call | solution.py:515
  27.4 0.6 %copy.11 = f32[1,2,64,128]{3,2,1,0:T(8,128)} copy(f32[1,2,64,128]{3,2,1,0:T(8,128)S(1)} %get-tuple-element.4) | data formatting | bytes 131072
  28.1 0.7 %copy.12 = f32[2,2,64,128]{3,2,1,0:T(8,128)} copy(f32[2,2,64,128]{3,2,1,0:T(8,128)S(1)} %get-tuple-element.5) | data formatting | bytes 262144
where the time goes:
time: 28.9 us; the launch traced here: 28.7 us
  Pallas kernels  26 us (90%)
  local copies, waits for them, and re-layouts  1.29 us (4%)
  other arithmetic  0.74 us (3%)
  between operations  0.64 us (2%)
    pallas_call x1, Pallas kernels, fused_device(): pl.pallas_call(fused_kernel, out_shape=(jax.ShapeDtypeStruct((1, 2, 64, 1...  26 us
    unnamed x2, local copies, waits for them, and re-layouts  1.29 us
    add x1, other arithmetic, fused_device(): sum((jnp.pad(rows, ((above, 7 - above - rows.shape[0]), (0, 128 - rows.sh...  0.74 us

commit v1 on v0

--- a/solution.py
+++ b/solution.py
@@ -235,8 +235,7 @@
 
 def fused_kernel(
     train_hbm, apply_hbm, settings, hard_out, easy_out,
-    cubes, expanded, upper0, upper1, upper2, upper3, lower0, lower1, lower2, lower3,
-    spectra, arrived_a, arrived_b, arrived_c, received_a, received_b,
+    cubes, table, gathered, spectra, arrived_a, arrived_b, arrived_c, received_a, received_b,
     part_a, part_b, part_c, inbox_a, inbox_b, inbox_c,
     merged_a, merged_b, merged_c, final_a, final_b, final_c,
     load_sem, send_sem, recv_sem, swap_send, swap_recv,
@@ -246,36 +245,35 @@
     groups = 8
     across = section + 1 - 2 * (section % 2)
     along = (section + 2) % 4
-    lhs = ((upper0, upper1, upper2, upper3), (lower0, lower1, lower2, lower3))
     loads = []
     for which, source in enumerate((train_hbm, apply_hbm)):
-        for k in range(4):
-            rows = pl.ds(2048 * k, 2048)
-            copy = pltpu.make_async_copy(
-                source.at[rows], cubes.at[which, rows], load_sem.at[which, k]
-            )
-            copy.start()
-            loads.append(copy)
+        for i in range(4):
+            for s in range(4):
+                copy = pltpu.make_async_copy(
+                    source.at[:, s, pl.ds(2 * i, 2), :],
+                    cubes.at[which, i, :, pl.ds(2 * s, 2), :],
+                    load_sem.at[which, i, s],
+                )
+                copy.start()
+                loads.append(copy)
+    depth, core = group // 2, group % 2
+    mirror = 1 - core
+    peers = [
+        2 * far + side
+        for far in (3 - depth, depth + 2 - 4 * (depth // 2), depth + 1 - 2 * (depth % 2))
+        for side in (core, mirror)
+    ] + [2 * depth + mirror]
     barrier = pltpu.get_barrier_semaphore()
-    for offset in range(1, groups):
-        pl.semaphore_signal(
-            barrier, inc=1, device_id=(section, (group + offset) % groups), device_id_type=MESH
-        )
+    for peer in peers:
+        pl.semaphore_signal(barrier, inc=1, device_id=(section, peer), device_id_type=MESH)
     for other in (across, along):
         pl.semaphore_signal(barrier, inc=1, device_id=(other, group), device_id_type=MESH)
 
-    block = (
-        lax.broadcasted_iota(jnp.int32, (16, 128), 1) // 8
-        == lax.broadcasted_iota(jnp.int32, (16, 128), 0)
+    spread = (
+        lax.broadcasted_iota(jnp.int32, (256, 1024), 1) % 512
+        - lax.broadcasted_iota(jnp.int32, (256, 1024), 0) * 2
+        == lax.broadcasted_iota(jnp.int32, (256, 1024), 1) // 512
     ).astype(jnp.float32).astype(jnp.bfloat16)
-    nothing = jnp.zeros((16, 128), jnp.bfloat16)
-    spread = jnp.concatenate(
-        [
-            jnp.concatenate([nothing] * j + [block] + [nothing] * (15 - j), axis=1)
-            for j in range(16)
-        ],
-        axis=0,
-    )
     pair = lax.broadcasted_iota(jnp.int32, (64, 128), 0) // 2
     bin_col = jnp.zeros((64, 128), jnp.int32)
     lag_col = jnp.zeros((64, 128), jnp.int32)
@@ -298,31 +296,24 @@
     stacked = jnp.concatenate(
         [first[:, :256], first[:, 256:], second[:, :256], second[:, 256:]], axis=0
     )
-    expanded[...] = jnp.dot(stacked, spread, preferred_element_type=jnp.float32)
-    diagonal = (lax.broadcasted_iota(jnp.int32, (16, 2048), 0) % 8) == (
-        lax.broadcasted_iota(jnp.int32, (16, 2048), 1) % 8
-    )
-
-    def fill(part, k):
-        for i in range(16):
-            row = 64 * k + 32 * part + 2 * i
-            upper = jnp.broadcast_to(expanded[row : row + 1, :], (8, 2048))
-            lower = jnp.broadcast_to(expanded[row + 1 : row + 2, :], (8, 2048))
-            both = jnp.where(diagonal, jnp.concatenate([upper, lower], axis=0), 0.0)
-            lhs[part][k][16 * i : 16 * i + 16, :] = both.astype(jnp.bfloat16)
+    expanded = jnp.dot(stacked, spread, preferred_element_type=jnp.float32).astype(jnp.bfloat16)
+    for p in range(2):
+        for k in range(4):
+            table[64 * p : 64 * p + 64, 512 * k : 512 * k + 512] = expanded[
+                64 * k : 64 * k + 64, 512 * p : 512 * p + 512
+            ]
 
     arrived = (arrived_a, arrived_b, arrived_c)
     sends = [[], [], [], [], []]
 
     def scatter(which, index, start, rows, landing):
         here = pl.ds(pl.multiple_of(rows * group, rows), rows)
-        for offset in range(1, groups):
-            target = (group + offset) % groups
+        for order, target in enumerate(peers):
             copy = pltpu.make_async_remote_copy(
                 src_ref=spectra.at[which, pl.ds(pl.multiple_of(32 * target + start, 16), rows)],
                 dst_ref=landing.at[here],
-                send_sem=send_sem.at[index, offset],
-                recv_sem=recv_sem.at[index, offset],
+                send_sem=send_sem.at[index, order],
+                recv_sem=recv_sem.at[index, order],
                 device_id=(section, target),
                 device_id_type=MESH,
             )
@@ -330,31 +321,28 @@
             sends[index].append(copy)
         landing[here, :] = spectra[which, pl.ds(pl.multiple_of(32 * group + start, 16), rows), :]
 
-    def transform(which, part):
-        total = None
-        for k in range(4):
-            if part == 0:
-                loads[4 * which + k].wait()
+    def transform(which):
+        for i in range(4):
+            for s in range(4):
+                loads[16 * which + 4 * i + s].wait()
             product = jnp.dot(
-                lhs[part][k][...], cubes[which, 2048 * k : 2048 * k + 2048, :],
+                table[...], cubes.at[which, i].reshape(2048, 256)[...],
                 preferred_element_type=jnp.float32,
             )
-            total = product if total is None else total + product
-        spectra[which, 256 * part : 256 * part + 256, :] = total.astype(jnp.bfloat16)
-
-    for k in range(4):
-        fill(0, k)
-    transform(0, 0)
+            for p in range(2):
+                for side in range(2):
+                    gathered[side, pl.ds(2 * i + p, 64, 8), :] = product[
+                        64 * p : 64 * p + 64, 128 * side : 128 * side + 128
+                    ]
+        spectra[which] = jnp.concatenate([gathered[0], gathered[1]], axis=1).astype(jnp.bfloat16)
+
+    transform(0)
     pl.semaphore_wait(barrier, groups + 1)
     scatter(0, 0, 0, 32, arrived_a)
-    for k in range(4):
-        fill(1, k)
-    transform(0, 1)
     scatter(0, 1, 256, 16, arrived_b)
     scatter(0, 2, 272, 16, arrived_c)
-    transform(1, 0)
+    transform(1)
     scatter(1, 3, 0, 32, received_a)
-    transform(1, 1)
     scatter(1, 4, 256, 32, received_b)
 
     lane = lax.broadcasted_iota(jnp.int32, (1, 128), 1) % 64
@@ -521,15 +509,15 @@
         in_specs=[pl.BlockSpec(memory_space=pltpu.HBM)] * 2 + [smem],
         out_specs=(vmem, vmem),
         scratch_shapes=[
-            pltpu.VMEM((2, 8192, 256), bf16),
-            pltpu.VMEM((256, 2048), f32),
-            *[pltpu.VMEM((256, 2048), bf16)] * 8,
+            pltpu.VMEM((2, 4, 256, 8, 256), bf16),
+            pltpu.VMEM((128, 2048), bf16),
+            pltpu.VMEM((2, 512, 128), f32),
             pltpu.VMEM((2, 512, 256), bf16),
             *held,
             pltpu.VMEM((256, 256), bf16),
             pltpu.VMEM((256, 256), bf16),
             *held, *held, *held, *held,
-            pltpu.SemaphoreType.DMA((2, 4)),
+            pltpu.SemaphoreType.DMA((2, 4, 4)),
             pltpu.SemaphoreType.DMA((5, 8)),
             pltpu.SemaphoreType.DMA((5, 8)),
             pltpu.SemaphoreType.DMA((3, 4)),
@@ -539,7 +527,7 @@
             collective_id=0, has_side_effects=True, vmem_limit_bytes=52 * 1024 * 1024
         ),
     )(
-        cube_train.reshape(8192, 256), cube_apply.reshape(8192, 256),
+        cube_train.reshape(256, 4, 8, 256), cube_apply.reshape(256, 4, 8, 256),
         settings,
     )
 

time: 28.9 us -> 30.6 us (1.059)
  Pallas kernels: 26 us -> 27.8 us
    pallas_call x1, Pallas kernels: 26 us -> 27.8 us  [fused_device(): pl.pallas_call(fused_kernel, out_shape=(jax.ShapeDtypeStruct((1, 2, 64, 1...]
where the time goes in v1:
time: 30.6 us; the launch traced here: 30.4 us
  Pallas kernels  27.8 us (91%)
  local copies, waits for them, and re-layouts  1.29 us (4%)
  other arithmetic  0.74 us (2%)
  between operations  0.64 us (2%)
    pallas_call x1, Pallas kernels, fused_device(): pl.pallas_call(fused_kernel, out_shape=(jax.ShapeDtypeStruct((1, 2, 64, 1...  27.8 us
    unnamed x2, local copies, waits for them, and re-layouts  1.29 us
    add x1, other arithmetic, fused_device(): sum((jnp.pad(rows, ((above, 7 - above - rows.shape[0]), (0, 128 - rows.sh...  0.74 us

profile of v1, /device:TPU:0, one launch (start us, length us, event | category | flops | bytes accessed | tf_op | source)
XLA Modules:
  0.0 30.4 jit_solution(18021734992971630547)
XLA Ops:
  0.6 0.7 %pad_add_fusion.settings = s32[7,128]{1,0:T(8,128)S(1)} fusion(s32[2,64]{1,0:T(2,128)} %param.13, s32[1,64]{1,0:T(1,128)} %param.12, s32[2,8]{1,0:T(2,128)} %bitcast.7, s32[1,16]{1,0:T(1,128)} %bitcast.8, s32[1,8]{1,0:T(1,128)} %bitcast.9), kind=kLoop, calls=%fused_computation | loop fusion | flops 3584 | bytes 4512 | tf_op jit(solution)/shard_map/add | solution.py:495
  1.4 27.8 %shard_map.86 = (f32[1,2,64,128]{3,2,1,0:T(8,128)S(1)}, f32[2,2,64,128]{3,2,1,0:T(8,128)S(1)}) custom-call(bf16[256,4,8,256]{3,2,1,0:T(8,128)(2,1)} %bitcast.5, bf16[256,4,8,256]{3,2,1,0:T(8,128)(2,1)} %bitcast.6, s32[7,128]{1,0:T(8,128)S(1)} %pad_add_fusion.settings), custom_call_target="tpu_custom_call" | custom-call | tf_op jit(solution)/shard_map/pallas_call | solution.py:503
  29.1 0.6 %copy.11 = f32[1,2,64,128]{3,2,1,0:T(8,128)} copy(f32[1,2,64,128]{3,2,1,0:T(8,128)S(1)} %get-tuple-element.4) | data formatting | bytes 131072
  29.8 0.7 %copy.12 = f32[2,2,64,128]{3,2,1,0:T(8,128)} copy(f32[2,2,64,128]{3,2,1,0:T(8,128)S(1)} %get-tuple-element.5) | data formatting | bytes 262144

commit v2 on v1

--- a/solution.py
+++ b/solution.py
@@ -233,6 +233,10 @@
     state["total"] = state["total"] + state["move"]
 
 
+def landed(ref, semaphore):
+    pltpu.make_async_copy(ref, ref, semaphore).wait()
+
+
 def fused_kernel(
     train_hbm, apply_hbm, settings, hard_out, easy_out,
     cubes, table, gathered, spectra, arrived_a, arrived_b, arrived_c, received_a, received_b,
@@ -245,17 +249,15 @@
     groups = 8
     across = section + 1 - 2 * (section % 2)
     along = (section + 2) % 4
-    loads = []
     for which, source in enumerate((train_hbm, apply_hbm)):
         for i in range(4):
             for s in range(4):
                 copy = pltpu.make_async_copy(
                     source.at[:, s, pl.ds(2 * i, 2), :],
                     cubes.at[which, i, :, pl.ds(2 * s, 2), :],
-                    load_sem.at[which, i, s],
+                    load_sem.at[which, i],
                 )
                 copy.start()
-                loads.append(copy)
     depth, core = group // 2, group % 2
     mirror = 1 - core
     peers = [
@@ -304,27 +306,26 @@
             ]
 
     arrived = (arrived_a, arrived_b, arrived_c)
-    sends = [[], [], [], [], []]
+    sent = tuple(ref.at[pl.ds(0, ref.shape[0] // 8 * 7)] for ref in arrived)
+    sent += tuple(ref.at[pl.ds(0, 224)] for ref in (received_a, received_b))
 
     def scatter(which, index, start, rows, landing):
         here = pl.ds(pl.multiple_of(rows * group, rows), rows)
-        for order, target in enumerate(peers):
+        for target in peers:
             copy = pltpu.make_async_remote_copy(
                 src_ref=spectra.at[which, pl.ds(pl.multiple_of(32 * target + start, 16), rows)],
                 dst_ref=landing.at[here],
-                send_sem=send_sem.at[index, order],
-                recv_sem=recv_sem.at[index, order],
+                send_sem=send_sem.at[index],
+                recv_sem=recv_sem.at[index],
                 device_id=(section, target),
                 device_id_type=MESH,
             )
             copy.start()
-            sends[index].append(copy)
         landing[here, :] = spectra[which, pl.ds(pl.multiple_of(32 * group + start, 16), rows), :]
 
     def transform(which):
         for i in range(4):
-            for s in range(4):
-                loads[16 * which + 4 * i + s].wait()
+            landed(cubes.at[which, i], load_sem.at[which, i])
             product = jnp.dot(
                 table[...], cubes.at[which, i].reshape(2048, 256)[...],
                 preferred_element_type=jnp.float32,
@@ -339,11 +340,9 @@
     transform(0)
     pl.semaphore_wait(barrier, groups + 1)
     scatter(0, 0, 0, 32, arrived_a)
+    transform(1)
     scatter(0, 1, 256, 16, arrived_b)
     scatter(0, 2, 272, 16, arrived_c)
-    transform(1)
-    scatter(1, 3, 0, 32, received_a)
-    scatter(1, 4, 256, 32, received_b)
 
     lane = lax.broadcasted_iota(jnp.int32, (1, 128), 1) % 64
     lists = [jnp.zeros((1, 128), jnp.int32)] * 3
@@ -370,23 +369,20 @@
 
     parts, inboxes = (part_a, part_b, part_c), (inbox_a, inbox_b, inbox_c)
     merges, finals = (merged_a, merged_b, merged_c), (final_a, final_b, final_c)
-    swaps = {}
 
     def swap(stage, index, origin, target):
         half_rows = 64 * len(PIECES[index])
-        swaps[stage, index] = []
         for half in range(2):
             rows = pl.ds(half_rows * half, half_rows)
             copy = pltpu.make_async_remote_copy(
                 src_ref=origin.at[rows],
                 dst_ref=target.at[rows],
-                send_sem=swap_send.at[index, 2 * stage + half],
-                recv_sem=swap_recv.at[index, 2 * stage + half],
+                send_sem=swap_send.at[index, stage],
+                recv_sem=swap_recv.at[index, stage],
                 device_id=((across, along)[(half + stage) % 2], group),
                 device_id_type=MESH,
             )
             copy.start()
-            swaps[stage, index].append(copy)
 
     channel = lax.broadcasted_iota(jnp.int32, (256, 128), 0)
     beam = lax.broadcasted_iota(jnp.int32, (256, 128), 1)
@@ -400,15 +396,17 @@
         rotations.append((cos512(angle)[0:1], cos512((angle + 384) & 511)[0:1]))
 
     for index in range(3):
-        for copy in sends[index]:
-            copy.wait_recv()
+        landed(sent[index], recv_sem.at[index])
         parts[index][...] = jnp.dot(
             selects[index], arrived[index][...], preferred_element_type=jnp.float32
         ).astype(jnp.bfloat16)
         swap(0, index, parts[index], inboxes[index])
     for index in range(3):
-        for copy in swaps[0, index]:
-            copy.wait_recv()
+        landed(sent[index], send_sem.at[index])
+    scatter(1, 3, 0, 32, received_a)
+    scatter(1, 4, 256, 32, received_b)
+    for index in range(3):
+        landed(inboxes[index], swap_recv.at[index, 0])
         merges[index][...] = parts[index][...] + inboxes[index][...]
         swap(1, index, merges[index], finals[index])
 
@@ -416,8 +414,7 @@
     for indices in ((0,), (1, 2)):
         states, mixers = [], {}
         for index in indices:
-            for copy in swaps[1, index]:
-                copy.wait_recv()
+            landed(finals[index], swap_recv.at[index, 1])
         for index in indices:
             kinds = PIECES[index]
             snapshot = merges[index][...] + finals[index][...]
@@ -461,8 +458,8 @@
                     axis=1,
                 ).astype(jnp.bfloat16)
 
-    for copy in sends[3] + sends[4]:
-        copy.wait_recv()
+    for index in (3, 4):
+        landed(sent[index], recv_sem.at[index])
     products = []
     for t in range(4):
         rows = jnp.concatenate(
@@ -483,9 +480,11 @@
             from_imag = product[16 * b + 8 : 16 * b + 16]
             out[at, 0, 8 * b : 8 * b + 8, :] = from_real[:, :128] + from_imag[:, 128:]
             out[at, 1, 8 * b : 8 * b + 8, :] = from_imag[:, :128] - from_real[:, 128:]
-    for copies in (*sends, *swaps.values()):
-        for copy in copies:
-            copy.wait_send()
+    for index in (3, 4):
+        landed(sent[index], send_sem.at[index])
+    for index in range(3):
+        for stage in range(2):
+            landed(inboxes[index], swap_send.at[index, stage])
 
 
 def fused_device(cube_train, cube_apply, hard_bins, easy_bins, stagger, hard_gates, easy_gates):
@@ -517,11 +516,11 @@
             pltpu.VMEM((256, 256), bf16),
             pltpu.VMEM((256, 256), bf16),
             *held, *held, *held, *held,
-            pltpu.SemaphoreType.DMA((2, 4, 4)),
-            pltpu.SemaphoreType.DMA((5, 8)),
-            pltpu.SemaphoreType.DMA((5, 8)),
-            pltpu.SemaphoreType.DMA((3, 4)),
-            pltpu.SemaphoreType.DMA((3, 4)),
+            pltpu.SemaphoreType.DMA((2, 4)),
+            pltpu.SemaphoreType.DMA((5,)),
+            pltpu.SemaphoreType.DMA((5,)),
+            pltpu.SemaphoreType.DMA((3, 2)),
+            pltpu.SemaphoreType.DMA((3, 2)),
         ],
         compiler_params=pltpu.CompilerParams(
             collective_id=0, has_side_effects=True, vmem_limit_bytes=52 * 1024 * 1024

time: 30.6 us -> 26.5 us (0.87)
  Pallas kernels: 27.8 us -> 23.6 us
    pallas_call x1, Pallas kernels: 27.8 us -> 23.6 us  [fused_device(): pl.pallas_call(fused_kernel, out_shape=(jax.ShapeDtypeStruct((1, 2, 64, 1...]
where the time goes in v2:
time: 26.5 us; the launch traced here: 26.3 us
  Pallas kernels  23.6 us (89%)
  local copies, waits for them, and re-layouts  1.29 us (5%)
  other arithmetic  0.74 us (3%)
  between operations  0.64 us (2%)
    pallas_call x1, Pallas kernels, fused_device(): pl.pallas_call(fused_kernel, out_shape=(jax.ShapeDtypeStruct((1, 2, 64, 1...  23.6 us
    unnamed x2, local copies, waits for them, and re-layouts  1.29 us
    add x1, other arithmetic, fused_device(): sum((jnp.pad(rows, ((above, 7 - above - rows.shape[0]), (0, 128 - rows.sh...  0.74 us

profile of v2, /device:TPU:0, one launch (start us, length us, event | category | flops | bytes accessed | tf_op | source)
XLA Modules:
  0.0 26.3 jit_solution(359442103437107871)
XLA Ops:
  0.6 0.7 %pad_add_fusion.settings = s32[7,128]{1,0:T(8,128)S(1)} fusion(s32[2,64]{1,0:T(2,128)} %param.13, s32[1,64]{1,0:T(1,128)} %param.12, s32[2,8]{1,0:T(2,128)} %bitcast.7, s32[1,16]{1,0:T(1,128)} %bitcast.8, s32[1,8]{1,0:T(1,128)} %bitcast.9), kind=kLoop, calls=%fused_computation | loop fusion | flops 3584 | bytes 4512 | tf_op jit(solution)/shard_map/add | solution.py:494
  1.4 23.6 %shard_map.86 = (f32[1,2,64,128]{3,2,1,0:T(8,128)S(1)}, f32[2,2,64,128]{3,2,1,0:T(8,128)S(1)}) custom-call(bf16[256,4,8,256]{3,2,1,0:T(8,128)(2,1)} %bitcast.5, bf16[256,4,8,256]{3,2,1,0:T(8,128)(2,1)} %bitcast.6, s32[7,128]{1,0:T(8,128)S(1)} %pad_add_fusion.settings), custom_call_target="tpu_custom_call" | custom-call | tf_op jit(solution)/shard_map/pallas_call | solution.py:502
  25.0 0.6 %copy.11 = f32[1,2,64,128]{3,2,1,0:T(8,128)} copy(f32[1,2,64,128]{3,2,1,0:T(8,128)S(1)} %get-tuple-element.4) | data formatting | bytes 131072
  25.7 0.7 %copy.12 = f32[2,2,64,128]{3,2,1,0:T(8,128)} copy(f32[2,2,64,128]{3,2,1,0:T(8,128)S(1)} %get-tuple-element.5) | data formatting | bytes 262144
